TPU v7x, 32 devices: a whole 2x2x4 slice. The times are simulated.
32 devices in a mesh: ctx: 8 (over z, y), kvh: 4 (over x, core).
Axes of the slice: x: 2, y: 2, z: 4, core: 2. Of those that a mesh axis runs over, the one named last changes fastest.
Arguments:
- queries: bfloat16 [4096, 3584], P('ctx', 'kvh'), may hold values from -384 to 384
- key_block: bfloat16 [4096, 512], P('ctx', 'kvh'), may hold values from -8 to 8
- value_block: bfloat16 [4096, 512], P('ctx', 'kvh'), may hold values from -6 to 6
- block_valid: int32 [8], replicated, may hold values from 2 to 512, as said below
- out_weight: bfloat16 [3584, 3584], P('kvh'), may hold values from -6 to 6
Outputs:
- projected: bfloat16 [4096, 3584], P(('ctx', 'kvh'))
Inputs may be any that keep to these rules, and one draw needn't show every extreme that they name: `block_valid`: every entry but the last equals 512.
All inputs are finite; a program needn't handle non-finite values.
Results may differ from a plain program's by a relative error of at most 0.01.
Values may be sent and summed in bfloat16 or wider, within the bound.
No kernel may reach another device: no remote copies, remote signals or barrier semaphores. Data moves between devices by JAX's collectives and lax.ppermute only.
A program may use at most 128 MiB of HBM per device.

v0:
```python
import jax
import jax.numpy as jnp
from jax import lax
from jax.sharding import PartitionSpec as P


def passed_along(block, axis, distance):
    devices = range(lax.axis_size(axis))
    route = [(i - distance, i) for i in devices if i - distance in devices]
    return lax.ppermute(block, axis, route)


def per_device(queries, key_block, value_block, block_valid, out_weight):
    row_count = queries.shape[0]
    head_size = key_block.shape[1]
    group_size = queries.shape[1] // head_size
    ctx_size = lax.axis_size("ctx")
    block_id = lax.axis_index("ctx")
    offsets = [1 << level_id for level_id in range((ctx_size - 1).bit_length())]
    position = jnp.arange(row_count, dtype=jnp.int32)
    key_list = [key_block]
    value_list = [value_block]
    mask_list = [
        (position[None, :] <= position[:, None]) & (position[None, :] < block_valid[block_id])
    ]
    for offset in offsets:
        moved_keys, moved_values = passed_along((key_block, value_block), "ctx", offset)
        key_list.append(moved_keys)
        value_list.append(moved_values)
    for offset in offsets:
        source = jnp.maximum(block_id - offset, 0)
        usable = (block_id - offset >= 0) & (position < block_valid[source])
        mask_list.append(jnp.broadcast_to(usable[None, :], (row_count, row_count)))
    keys_cat = jnp.concatenate(key_list, axis=0)
    values_cat = jnp.concatenate(value_list, axis=0)
    allowed = jnp.concatenate(mask_list, axis=1)
    query_heads = queries.reshape(row_count, group_size, head_size)
    score_scale = head_size ** (-0.5)
    results = []
    for head_id in range(group_size):
        scores = (
            lax.dot_general(
                query_heads[:, head_id, :],
                keys_cat,
                (((1,), (1,)), ((), ())),
                preferred_element_type=jnp.float32,
            )
            * score_scale
        )
        scores = jnp.where(allowed, scores, -1e30)
        row_max = jnp.max(scores, axis=-1, keepdims=True)
        numerators = jnp.where(allowed, jnp.exp(scores - row_max), 0.0)
        row_total = jnp.sum(numerators, axis=-1)
        weights = numerators.astype(jnp.bfloat16)
        mixture = (
            jnp.dot(weights, values_cat, preferred_element_type=jnp.float32) / row_total[:, None]
        )
        results.append(mixture.astype(jnp.bfloat16))
    attended = jnp.concatenate(results, axis=1)
    return lax.psum_scatter(
        jnp.dot(attended, out_weight, preferred_element_type=jnp.float32).astype(jnp.bfloat16),
        "kvh",
        scatter_dimension=0,
        tiled=True,
    )


def solution(mesh):
    return jax.shard_map(
        per_device,
        mesh=mesh,
        in_specs=(P("ctx", "kvh"), P("ctx", "kvh"), P("ctx", "kvh"), P(), P("kvh", None)),
        out_specs=P(("ctx", "kvh"), None),
        check_vma=False,
    )
```

profile of v0, /device:TPU:0, one launch (start us, length us, event | category | flops | bytes accessed | tf_op | source)
XLA Modules:
  0.0 125.7 jit_solution(552450410211709097)
XLA Ops:
  6.5 0.0 reduce-scatter.2.cloned.1.call-start
  6.5 4.9 %collective-permute-start = (bf16[512,128]{1,0:T(8,128)(2,1)}, bf16[512,128]{1,0:T(8,128)(2,1)S(1)}, u32[]{:S(2)}, u32[]{:S(2)}) collective-permute-start(bf16[512,128]{1,0:T(8,128)(2,1)} %param.6), channel_id=1, source_target_pairs={{0,4},{4,8},{8,12},{12,16},{16,20},{20,24},{24,28},{1,5},{5,9},{9,... | collective-permute-start | bytes 393224 | tf_op jit(solution)/shard_map/ppermute | solution.py:10
  11.4 3.5 %collective-permute-start.1 = (bf16[512,128]{1,0:T(8,128)(2,1)}, bf16[512,128]{1,0:T(8,128)(2,1)S(1)}, u32[]{:S(2)}, u32[]{:S(2)}) collective-permute-start(bf16[512,128]{1,0:T(8,128)(2,1)} %param.6), channel_id=1, source_target_pairs={{0,8},{4,12},{8,16},{12,20},{16,24},{20,28},{1,9},{5,13},{9,17},{1... | collective-permute-start | bytes 393224 | tf_op jit(solution)/shard_map/ppermute | solution.py:10
  14.9 4.5 %collective-permute-start.2 = (bf16[512,128]{1,0:T(8,128)(2,1)}, bf16[512,128]{1,0:T(8,128)(2,1)S(1)}, u32[]{:S(2)}, u32[]{:S(2)}) collective-permute-start(bf16[512,128]{1,0:T(8,128)(2,1)} %param.6), channel_id=1, source_target_pairs={{0,16},{4,20},{8,24},{12,28},{1,17},{5,21},{9,25},{13,29},{2,18},{... | collective-permute-start | bytes 393224 | tf_op jit(solution)/shard_map/ppermute | solution.py:10
  19.4 1.9 %collective-permute-start.3 = (bf16[512,128]{1,0:T(8,128)(2,1)}, bf16[512,128]{1,0:T(8,128)(2,1)S(1)}, u32[]{:S(2)}, u32[]{:S(2)}) collective-permute-start(bf16[512,128]{1,0:T(8,128)(2,1)} %param.7), channel_id=1, source_target_pairs={{0,4},{4,8},{8,12},{12,16},{16,20},{20,24},{24,28},{1,5},{5,9},{9,... | collective-permute-start | bytes 393224 | tf_op jit(solution)/shard_map/ppermute | solution.py:10
  21.3 1.8 %collective-permute-start.4 = (bf16[512,128]{1,0:T(8,128)(2,1)}, bf16[512,128]{1,0:T(8,128)(2,1)S(1)}, u32[]{:S(2)}, u32[]{:S(2)}) collective-permute-start(bf16[512,128]{1,0:T(8,128)(2,1)} %param.7), channel_id=1, source_target_pairs={{0,8},{4,12},{8,16},{12,20},{16,24},{20,28},{1,9},{5,13},{9,17},{1... | collective-permute-start | bytes 393224 | tf_op jit(solution)/shard_map/ppermute | solution.py:10
  23.2 0.9 constant_dynamic-update-slice_fusion.3
  24.1 0.9 constant_dynamic-update-slice_fusion.7
  25.0 1.5 %fusion.130 = (s32[1]{0:T(128)}, s32[1]{0:T(128)}, s32[1]{0:T(128)}, s32[1]{0:T(128)}) fusion(s32[8]{0:T(128)} %param.8, s32[]{:T(128)S(6)} %select_n.49, s32[]{:T(128)S(6)} %max.9, s32[]{:T(128)S(6)} %max.11, s32[]{:T(128)S(6)} %max.10), kind=kLoop, calls=%fused_computation.117 | loop fusion | bytes 48 | tf_op jit(solution)/shard_map/dynamic_slice | solution.py:24
  26.5 0.6 iota_compare_fusion.4
  27.2 0.1 fusion.98
  27.3 0.7 fusion.106
  28.0 0.6 fusion.107
  28.7 0.6 fusion.108
  29.3 1.5 %copy.6 = bf16[512,896]{0,1:T(8,128)(2,1)S(1)} copy(bf16[512,896]{1,0:T(8,128)(2,1)} %param.5) | data formatting | bytes 1835008 | tf_op args[0]
  30.7 0.0 collective-permute-done
  30.7 1.4 %collective-permute-start.5 = (bf16[512,128]{1,0:T(8,128)(2,1)}, bf16[512,128]{1,0:T(8,128)(2,1)S(1)}, u32[]{:S(2)}, u32[]{:S(2)}) collective-permute-start(bf16[512,128]{1,0:T(8,128)(2,1)} %param.7), channel_id=1, source_target_pairs={{0,16},{4,20},{8,24},{12,28},{1,17},{5,21},{9,25},{13,29},{2,18},{... | collective-permute-start | bytes 393224 | tf_op jit(solution)/shard_map/ppermute | solution.py:10
  32.2 0.0 collective-permute-done.1
  32.2 0.0 collective-permute-done.2
  32.3 0.7 fusion.100
  33.0 0.7 fusion.101
  33.7 0.7 fusion.102
  34.4 0.7 fusion.103
  35.0 2.6 %fusion.104 = f32[2048,512]{1,0:T(8,128)} fusion(bf16[2048,128]{1,0:T(8,128)(2,1)S(1)} %constant_dynamic-update-slice_fusion, bf16[512,7,128]{0,2,1:T(8,128)(2,1)S(1)} %bitcast.174), kind=kOutput, calls=%fused_computation.78 | convolution fusion | flops 268435456 | bytes 4849664 | tf_op jit(solution)/shard_map/dot_general | solution.py:42
  37.7 2.7 %fusion.105 = f32[2048,512]{1,0:T(8,128)} fusion(bf16[2048,128]{1,0:T(8,128)(2,1)S(1)} %constant_dynamic-update-slice_fusion, bf16[512,7,128]{0,2,1:T(8,128)(2,1)S(1)} %bitcast.175), kind=kOutput, calls=%fused_computation.80 | convolution fusion | flops 268435456 | bytes 4849664 | tf_op jit(solution)/shard_map/dot_general | solution.py:42
  40.3 10.7 %fusion.6 = (f32[512]{0:T(512)S(1)}, f32[512]{0:T(512)S(1)}, f32[512]{0:T(512)S(1)}, f32[512]{0:T(512)S(1)}, f32[512]{0:T(512)S(1)}, /*index=5*/f32[512]{0:T(512...) fusion(f32[2048,512]{1,0:T(8,128)S(1)} %fusion.100, f32[2048,512]{1,0:T(8,128)S(1)} %fusion.101, ...), kind=kOutput, calls=%fused_computation.22 | convolution fusion | flops 293597696 | bytes 31346688 | tf_op jit(solution)/shard_map/dot_general | solution.py:42
  51.1 0.0 copy-start.1
  51.1 9.4 %fusion.19 = (f32[512]{0:T(512)S(1)}, f32[512]{0:T(512)S(1)}, f32[512]{0:T(512)S(1)}, f32[512]{0:T(512)S(1)}, f32[512]{0:T(512)S(1)}, /*index=5*/f32[512]{0:T(512)S(1)}, f32[512]{0:T(512)S(1)}) fusion(pred[512,2048]{0,1:T(32,128)(4,1)S(1)} %get-tuple-element.19, f32[2048,512]{1,0:T(8,128)} %get-tuple-element.24, f32[512]{0:T(512)S(1)} %get-tuple-element.12, ...), kind=kLoop, calls=%fused_computation.35 | loop fusion | flops 36696576 | bytes 30437376 | tf_op jit(solution)/shard_map/reduce_sum | solution.py:53
  60.5 0.0 collective-permute-done.3
  60.6 0.0 collective-permute-done.4
  60.6 0.0 collective-permute-done.5
  60.6 0.0 copy-done.1
  60.6 0.0 copy-start
  60.7 1.7 %fusion.41 = bf16[512,896]{1,0:T(8,128)(2,1)S(1)} fusion(bf16[2048,128]{1,0:T(8,128)(2,1)S(1)} %constant_dynamic-update-slice_fusion.4, pred[512,2048]{0,1:T(32,128)(4,1)S(1)} %get-tuple-element.19, f32[2048,512]{1,0:T(8,128)S(1)} %copy-done.1, f32[512]{0:T(512)S(1)} %get-tuple-element.18, f32[512]{0:T(512)S(1)} %get-tuple-element.11), kind=kOutput, calls=%fused_computation.46 | convolution fusion | flops 273809408 | bytes 5902336 | tf_op jit(solution)/shard_map/dot_general | solution.py:56
  62.3 0.5 copy-done
  62.8 1.7 %fusion.50 = bf16[512,896]{1,0:T(8,128)(2,1)S(1)} fusion(bf16[512,896]{1,0:T(8,128)(2,1)S(1)} %fusion.41, bf16[2048,128]{1,0:T(8,128)(2,1)S(1)} %constant_dynamic-update-slice_fusion.4, pred[512,2048]{0,1:T(32,128)(4,1)S(1)} %get-tuple-element.19, f32[2048,512]{1,0:T(8,128)S(1)} %copy-done, f32[512]{0:T(512)S(1)} %get-tuple-element.17, ...), kind=kOutput, calls=%fused_computation.49 | convolution fusion | flops 273809408 | bytes 5902336 | tf_op jit(solution)/shard_map/dot_general | solution.py:56
  64.5 1.7 %fusion.59 = bf16[512,896]{1,0:T(8,128)(2,1)S(1)} fusion(bf16[512,896]{1,0:T(8,128)(2,1)S(1)} %fusion.50, bf16[2048,128]{1,0:T(8,128)(2,1)S(1)} %constant_dynamic-update-slice_fusion.4, pred[512,2048]{0,1:T(32,128)(4,1)S(1)} %get-tuple-element.19, f32[2048,512]{1,0:T(8,128)S(1)} %fusion.103, f32[512]{0:T(512)S(1)} %get-tuple-element.16, ...), kind=kOutput, calls=%fused_computation.52 | convolution fusion | flops 273809408 | bytes 5902336 | tf_op jit(solution)/shard_map/dot_general | solution.py:56
  66.2 1.7 %fusion.68 = bf16[512,896]{1,0:T(8,128)(2,1)S(1)} fusion(bf16[512,896]{1,0:T(8,128)(2,1)S(1)} %fusion.59, bf16[2048,128]{1,0:T(8,128)(2,1)S(1)} %constant_dynamic-update-slice_fusion.4, pred[512,2048]{0,1:T(32,128)(4,1)S(1)} %get-tuple-element.19, f32[2048,512]{1,0:T(8,128)S(1)} %fusion.102, f32[512]{0:T(512)S(1)} %get-tuple-element.15, ...), kind=kOutput, calls=%fused_computation.55 | convolution fusion | flops 273809408 | bytes 5902336 | tf_op jit(solution)/shard_map/dot_general | solution.py:56
  67.9 1.7 %fusion.77 = bf16[512,896]{1,0:T(8,128)(2,1)S(1)} fusion(bf16[512,896]{1,0:T(8,128)(2,1)S(1)} %fusion.68, bf16[2048,128]{1,0:T(8,128)(2,1)S(1)} %constant_dynamic-update-slice_fusion.4, pred[512,2048]{0,1:T(32,128)(4,1)S(1)} %get-tuple-element.19, f32[2048,512]{1,0:T(8,128)S(1)} %fusion.101, f32[512]{0:T(512)S(1)} %get-tuple-element.14, ...), kind=kOutput, calls=%fused_computation.58 | convolution fusion | flops 273809408 | bytes 5902336 | tf_op jit(solution)/shard_map/dot_general | solution.py:56
  69.6 0.0 copy-start.2
  69.6 0.0 slice-start
  69.6 1.7 %fusion.86 = bf16[512,896]{1,0:T(8,128)(2,1)S(1)} fusion(bf16[512,896]{1,0:T(8,128)(2,1)S(1)} %fusion.77, bf16[2048,128]{1,0:T(8,128)(2,1)S(1)} %constant_dynamic-update-slice_fusion.4, pred[512,2048]{0,1:T(32,128)(4,1)S(1)} %get-tuple-element.19, f32[2048,512]{1,0:T(8,128)S(1)} %fusion.100, f32[512]{0:T(512)S(1)} %get-tuple-element.13, ...), kind=kOutput, calls=%fused_computation.61 | convolution fusion | flops 273809408 | bytes 5902336 | tf_op jit(solution)/shard_map/dot_general | solution.py:56
  71.3 0.0 slice-start.1
  71.3 0.5 copy-done.2
  71.8 1.7 %fusion.95 = bf16[512,896]{1,0:T(8,128)(2,1)S(1)} fusion(bf16[512,896]{1,0:T(8,128)(2,1)S(1)} %fusion.86, bf16[2048,128]{1,0:T(8,128)(2,1)S(1)} %constant_dynamic-update-slice_fusion.4, pred[512,2048]{0,1:T(32,128)(4,1)S(1)} %get-tuple-element.19, f32[2048,512]{1,0:T(8,128)S(1)} %copy-done.2, f32[512]{0:T(512)S(1)} %get-tuple-element.12, ...), kind=kOutput, calls=%fused_computation.64 | convolution fusion | flops 273809408 | bytes 5902336 | tf_op jit(solution)/shard_map/dot_general | solution.py:56
  73.4 0.0 slice-done
  73.4 0.4 slice-done.1
  73.9 5.5 %convolution_convert_fusion = bf16[512,3584]{1,0:T(8,128)(2,1)} fusion(bf16[512,896]{1,0:T(8,128)(2,1)S(1)} %fusion.95, bf16[896,3584]{1,0:T(8,128)(2,1)S(1)} %bitcast.178), kind=kOutput, calls=%fused_computation | convolution fusion | flops 3290169344 | bytes 11010048 | tf_op jit(solution)/shard_map/dot_general | solution.py:61
  79.4 0.0 reduce-scatter.2.cloned.1.call-update
  79.4 39.5 %reduce-scatter.2.cloned.1.call-done = bf16[128,3584]{1,0:T(8,128)(2,1)} async-done(((bf16[512,3584]{1,0:T(8,128)(2,1)}), bf16[128,3584]{1,0:T(8,128)(2,1)}) %reduce-scatter.2.cloned.1.call-update) | async-done | bytes 917520 | tf_op jit(solution)/shard_map/reduce_scatter | solution.py:60
  (10 shorter events, 0.1 us)
Async XLA Ops:
  6.5 112.3 %reduce-scatter.2.cloned.1.call-start = ((), (), s32[]{:S(2)}) async-start(), calls=%async_computation.1 | async-start | bytes 4587520 | tf_op jit(solution)/shard_map/reduce_scatter | solution.py:60
  6.5 24.2 %collective-permute-start = (bf16[512,128]{1,0:T(8,128)(2,1)}, bf16[512,128]{1,0:T(8,128)(2,1)S(1)}, u32[]{:S(2)}, u32[]{:S(2)}) collective-permute-start(bf16[512,128]{1,0:T(8,128)(2,1)} %param.6), channel_id=1, source_target_pairs={{0,4},{4,8},{8,12},{12,16},{16,20},{20,24},{24,28},{1,5},{5,9},{9,... | collective-permute-start | bytes 393224 | tf_op jit(solution)/shard_map/ppermute | solution.py:10
  11.4 20.8 %collective-permute-start.1 = (bf16[512,128]{1,0:T(8,128)(2,1)}, bf16[512,128]{1,0:T(8,128)(2,1)S(1)}, u32[]{:S(2)}, u32[]{:S(2)}) collective-permute-start(bf16[512,128]{1,0:T(8,128)(2,1)} %param.6), channel_id=1, source_target_pairs={{0,8},{4,12},{8,16},{12,20},{16,24},{20,28},{1,9},{5,13},{9,17},{1... | collective-permute-start | bytes 393224 | tf_op jit(solution)/shard_map/ppermute | solution.py:10
  14.9 17.3 %collective-permute-start.2 = (bf16[512,128]{1,0:T(8,128)(2,1)}, bf16[512,128]{1,0:T(8,128)(2,1)S(1)}, u32[]{:S(2)}, u32[]{:S(2)}) collective-permute-start(bf16[512,128]{1,0:T(8,128)(2,1)} %param.6), channel_id=1, source_target_pairs={{0,16},{4,20},{8,24},{12,28},{1,17},{5,21},{9,25},{13,29},{2,18},{... | collective-permute-start | bytes 393224 | tf_op jit(solution)/shard_map/ppermute | solution.py:10
  19.4 41.1 %collective-permute-start.3 = (bf16[512,128]{1,0:T(8,128)(2,1)}, bf16[512,128]{1,0:T(8,128)(2,1)S(1)}, u32[]{:S(2)}, u32[]{:S(2)}) collective-permute-start(bf16[512,128]{1,0:T(8,128)(2,1)} %param.7), channel_id=1, source_target_pairs={{0,4},{4,8},{8,12},{12,16},{16,20},{20,24},{24,28},{1,5},{5,9},{9,... | collective-permute-start | bytes 393224 | tf_op jit(solution)/shard_map/ppermute | solution.py:10
  21.3 39.2 %collective-permute-start.4 = (bf16[512,128]{1,0:T(8,128)(2,1)}, bf16[512,128]{1,0:T(8,128)(2,1)S(1)}, u32[]{:S(2)}, u32[]{:S(2)}) collective-permute-start(bf16[512,128]{1,0:T(8,128)(2,1)} %param.7), channel_id=1, source_target_pairs={{0,8},{4,12},{8,16},{12,20},{16,24},{20,28},{1,9},{5,13},{9,17},{1... | collective-permute-start | bytes 393224 | tf_op jit(solution)/shard_map/ppermute | solution.py:10
  30.7 29.8 %collective-permute-start.5 = (bf16[512,128]{1,0:T(8,128)(2,1)}, bf16[512,128]{1,0:T(8,128)(2,1)S(1)}, u32[]{:S(2)}, u32[]{:S(2)}) collective-permute-start(bf16[512,128]{1,0:T(8,128)(2,1)} %param.7), channel_id=1, source_target_pairs={{0,16},{4,20},{8,24},{12,28},{1,17},{5,21},{9,25},{13,29},{2,18},{... | collective-permute-start | bytes 393224 | tf_op jit(solution)/shard_map/ppermute | solution.py:10
  51.1 9.6 %copy-start.1 = (f32[2048,512]{1,0:T(8,128)S(1)}, f32[2048,512]{1,0:T(8,128)}, u32[]{:S(2)}) copy-start(f32[2048,512]{1,0:T(8,128)} %fusion.105) | copy-start | bytes 12582916
  60.6 2.2 %copy-start = (f32[2048,512]{1,0:T(8,128)S(1)}, f32[2048,512]{1,0:T(8,128)}, u32[]{:S(2)}) copy-start(f32[2048,512]{1,0:T(8,128)} %fusion.104) | copy-start | bytes 12582916
  69.6 2.2 %copy-start.2 = (f32[2048,512]{1,0:T(8,128)S(1)}, f32[2048,512]{1,0:T(8,128)}, u32[]{:S(2)}) copy-start(f32[2048,512]{1,0:T(8,128)} %get-tuple-element.24) | copy-start | bytes 12582916
  69.6 3.9 %slice-start = ((s8[6422528]{0:T(1024)(128)(4,1)}), s8[4194304]{0:T(1024)(128)(4,1)S(1)}, s32[]{:S(2)}) async-start(s8[6422528]{0:T(1024)(128)(4,1)} %bitcast.177), calls=%async_computation.2 | async-start | bytes 8388608
  71.3 2.6 %slice-start.1 = ((s8[6422528]{0:T(1024)(128)(4,1)}), s8[2228224]{0:T(1024)(128)(4,1)S(1)}, s32[]{:S(2)}) async-start(s8[6422528]{0:T(1024)(128)(4,1)} %bitcast.177), calls=%async_computation.3 | async-start | bytes 4456448
Sparse Core Ops, SparseCore 0:
  79.5 39.3 reduce-scatter.1
where the time goes:
time: 126 us
  waiting for transfers between devices  39.5 us (31%)
  matrix products  36 us (29%)
  starting transfers between devices  18 us (14%)
  between operations  13.7 us (11%)
  other arithmetic  12.1 us (10%)
  local copies, waits for them, and re-layouts  6.35 us (5%)
    reduce_scatter x1, waiting for transfers between devices, per_device(): lax.psum_scatter(jnp.dot(attended, out_weight, preferred_element_type=jnp...  39.5 us
    dot_general x7, matrix products, per_device(): lax.dot_general(query_heads[:, head_id, :], keys_cat, (((1,), (1,)), ((),...  18.8 us
    ppermute x6, starting transfers between devices, passed_along(): return lax.ppermute(block, axis, route)  18 us
    dot_general x7, matrix products, per_device(): jnp.dot(weights, values_cat, preferred_element_type=jnp.float32)  11.7 us
    reduce_sum x1, other arithmetic, per_device(): row_total = jnp.sum(numerators, axis=-1)  9.45 us
    dot_general x1, matrix products, per_device(): jnp.dot(attended, out_weight, preferred_element_type=jnp.float32)  5.5 us
    unnamed x17, local copies, waits for them, and re-layouts  4.81 us
  transfers between devices with their start and end apart: 7, of which 1 were waited for; matrix products, arithmetic and copies ran while one was open for 28% of the time, Pallas kernels for 0%

commit v1 on v0

v1 whole, which is shorter than its diff:
```python
import functools
import math

import jax
import jax.numpy as jnp
from jax import lax
from jax.experimental import pallas as pl
from jax.experimental.pallas import tpu as pltpu
from jax.sharding import PartitionSpec as P

F32 = jnp.float32
BF16 = jnp.bfloat16
LOW = -1e30
MIB = 1 << 20
CHUNKS = 2


def stack_heads(rows, head_size):
    heads = rows.shape[1] // head_size
    return jnp.concatenate(
        [rows[:, i * head_size : (i + 1) * head_size] for i in range(heads)], axis=0
    )


def unstack_heads(rows, heads):
    count = rows.shape[0] // heads
    return jnp.concatenate([rows[i * count : (i + 1) * count] for i in range(heads)], axis=1)


def block_step(q, keys, values, state, scale, limit=None, present=None):
    scores = lax.dot_general(q, keys, (((1,), (1,)), ((), ())), preferred_element_type=F32)
    if limit is not None:
        column = lax.broadcasted_iota(jnp.int32, scores.shape, 1)
        scores = jnp.where(column < limit, scores, LOW)
    block_max = jnp.max(scores, axis=1, keepdims=True)
    if present is not None:
        block_max = jnp.where(present, block_max, LOW)
    row_max = block_max if state is None else jnp.maximum(state[0], block_max)
    shift = row_max if present is None else jnp.where(present, row_max, -LOW)
    weights = jnp.exp2((scores - shift) * scale).astype(BF16)
    total = jnp.dot(weights, values, preferred_element_type=F32)
    if state is not None:
        total = total + state[1] * jnp.exp2((state[0] - row_max) * scale)
    return row_max, total


def gather_queries(q_ref, starts, count, head_size):
    return jnp.concatenate(
        [stack_heads(q_ref[pl.ds(start, count), :], head_size) for start in starts], axis=0
    )


def attend(q, state, k_refs, v_refs, wide, scale, limit, presents):
    block, head_size = k_refs[0].shape
    for i, v_ref in enumerate(v_refs):
        wide[i * block : (i + 1) * block, :head_size] = v_ref[...]
        wide[i * block : (i + 1) * block, head_size:] = jnp.ones((block, head_size), BF16)
    for i, k_ref in enumerate(k_refs):
        state = block_step(
            q,
            k_ref[...],
            wide[i * block : (i + 1) * block, :],
            state,
            scale,
            limit=limit if i == 0 else None,
            present=None if presents[i] is None else presents[i] > 0,
        )
    return state


def row_limits(starts, count, heads, valid):
    row = lax.broadcasted_iota(jnp.int32, (count, 1), 0)
    return jnp.concatenate(
        [jnp.minimum(row + (start + 1), valid) for start in starts for _ in range(heads)], axis=0
    )


def row_starts(turn, count, offset, piece):
    kvh_size = lax.axis_size("kvh")
    kvh_id = lax.axis_index("kvh")
    groups = kvh_size // 2
    lane = lax.rem(kvh_id, 2)
    target = lax.rem(lax.div(kvh_id, 2) + turn, groups)
    return [
        pl.multiple_of((target * 2 + part) * count + offset, piece) for part in (1 - lane, lane)
    ]


def stage_kernel(*refs):
    count = len(refs) // 2
    sems = refs[-1]
    copies = [
        pltpu.make_async_copy(refs[i], refs[count + i], sems.at[i]) for i in range(count)
    ]
    for copy in copies:
        copy.start()
    for copy in copies:
        copy.wait()


def stage(*arrays):
    return pl.pallas_call(
        stage_kernel,
        in_specs=[pl.BlockSpec(memory_space=pltpu.HBM)] * len(arrays),
        out_specs=[pl.BlockSpec(memory_space=pltpu.VMEM)] * len(arrays),
        out_shape=[jax.ShapeDtypeStruct(x.shape, x.dtype) for x in arrays],
        scratch_shapes=[pltpu.SemaphoreType.DMA((len(arrays),))],
        cost_estimate=pl.CostEstimate(
            flops=0, bytes_accessed=sum(2 * x.size for x in arrays), transcendentals=0
        ),
        compiler_params=pltpu.CompilerParams(vmem_limit_bytes=12 * MIB),
        name="stage",
    )(*arrays)


def kernel_body(mode, scale, levels, turn, offset, count, *refs):
    if mode != "late":
        block_valid, refs = refs[0], refs[1:]
    q_ref, refs = refs[0], refs[1:]
    if mode == "late":
        state_ref, refs = refs[0], refs[1:]
    if mode != "early":
        w_ref, refs = refs[0], refs[1:]
    blocks = len(levels)
    k_refs, refs = refs[:blocks], refs[blocks:]
    v_refs, refs = refs[:blocks], refs[blocks:]
    wide = refs[-1]
    head_size = k_refs[0].shape[1]
    heads = q_ref.shape[1] // head_size
    block_id = lax.axis_index("ctx")
    rows_of = q_ref.shape[0] // lax.axis_size("kvh")
    starts = row_starts(turn, rows_of, offset, count)
    q = gather_queries(q_ref, starts, count, head_size)
    presents = [None if level is None else block_id - (1 << level) + 1 for level in levels]
    limit, state = None, None
    if mode == "late":
        old = state_ref[:, :, offset : offset + count, :].reshape(2 * heads * count, -1)
        state = old[:, 3 * head_size // 2 :][:, :1], old
        state = (
            state[0],
            jnp.concatenate(
                [
                    old[:, :head_size],
                    jnp.broadcast_to(old[:, head_size:][:, :1], (old.shape[0], head_size)),
                ],
                axis=1,
            ),
        )
    else:
        limit = row_limits(starts, count, heads, block_valid[block_id])
    row_max, total = attend(q, state, k_refs, v_refs, wide, scale, limit, presents)
    if mode == "early":
        lane = lax.broadcasted_iota(jnp.int32, (1, 2 * head_size), 1)
        packed = jnp.where(lane < 3 * head_size // 2, total, row_max)
        refs[0][...] = packed.reshape(refs[0].shape)
        return
    mixed = (total[:, :head_size] / total[:, head_size:]).astype(BF16)
    half = heads * count
    mixed = jnp.concatenate([unstack_heads(mixed[i * half : (i + 1) * half], heads) for i in range(2)], axis=0)
    out = jnp.dot(mixed, w_ref[...], preferred_element_type=F32).astype(BF16)
    for part in range(2):
        refs[part][...] = out[part * count : (part + 1) * count]


def call(mode, scale, levels, turn, offset, count, block_valid, q, state, weight, keys, values):
    head_size = keys[0].shape[1]
    block = keys[0].shape[0]
    heads = q.shape[1] // head_size
    blocks = len(levels)
    operands = [q]
    if mode == "late":
        operands.append(state)
    if mode != "early":
        operands.append(weight)
    operands += list(keys) + list(values)
    if mode == "early":
        shapes = [jax.ShapeDtypeStruct((2, heads, count, 2 * head_size), F32)]
    else:
        shapes = [jax.ShapeDtypeStruct((count, weight.shape[1]), BF16)] * 2
    flops = 2 * 2 * count * q.shape[1] * blocks * block * 2
    if mode != "early":
        flops += 4 * count * weight.size
    vmem = pl.BlockSpec(memory_space=pltpu.VMEM)
    smem = pl.BlockSpec(memory_space=pltpu.SMEM)
    scalars = [] if mode == "late" else [block_valid]
    return pl.pallas_call(
        functools.partial(kernel_body, mode, scale, levels, turn, offset, count),
        in_specs=[smem] * len(scalars) + [vmem] * len(operands),
        out_specs=[vmem] * len(shapes),
        out_shape=shapes,
        scratch_shapes=[pltpu.VMEM((blocks * block, 2 * head_size), BF16)],
        cost_estimate=pl.CostEstimate(
            flops=flops,
            bytes_accessed=sum(x.size * x.dtype.itemsize for x in operands),
            transcendentals=2 * count * heads * blocks * block,
        ),
        compiler_params=pltpu.CompilerParams(vmem_limit_bytes=32 * MIB),
    )(*scalars, *operands)


def finish_kernel(keep_ref, got_ref, *refs):
    out_ref = refs[-1]
    start = 0
    for ref in refs[:-1]:
        stop = start + ref.shape[0]
        total = keep_ref[start:stop, :].astype(F32) + got_ref[start:stop, :].astype(F32)
        for i in range(ref.shape[1] // keep_ref.shape[1]):
            width = keep_ref.shape[1]
            total = total + ref[:, i * width : (i + 1) * width].astype(F32)
        out_ref[start:stop, :] = total.astype(BF16)
        start = stop


def finish(keep, got, others):
    return pl.pallas_call(
        finish_kernel,
        in_specs=[pl.BlockSpec(memory_space=pltpu.VMEM)] * (2 + len(others)),
        out_specs=pl.BlockSpec(memory_space=pltpu.VMEM),
        out_shape=jax.ShapeDtypeStruct(keep.shape, BF16),
        cost_estimate=pl.CostEstimate(flops=3 * keep.size, bytes_accessed=8 * keep.size, transcendentals=0),
        compiler_params=pltpu.CompilerParams(vmem_limit_bytes=16 * MIB),
        name="finish",
    )(keep, got, *others)


def cycle(block, axis, distance, first=0):
    count = lax.axis_size(axis) - first
    return lax.ppermute(
        block, axis, [(first + i, first + (i + distance) % count) for i in range(count)]
    )


def swapped(block, axis):
    return lax.ppermute(block, axis, [(i, i ^ 1) for i in range(lax.axis_size(axis))])


def per_device(queries, key_block, value_block, block_valid, out_weight):
    head_size = key_block.shape[1]
    ctx_size = lax.axis_size("ctx")
    kvh_size = lax.axis_size("kvh")
    block_id = lax.axis_index("ctx")
    levels = (ctx_size - 1).bit_length()
    scale = head_size ** (-0.5) * math.log2(math.e)
    count = queries.shape[0] // kvh_size
    groups = kvh_size // 2

    keys, values = [None] * levels, [None] * levels
    odd = block_id % 2 == 1
    keys[1] = cycle(key_block, "ctx", 2)
    values[1] = cycle(value_block, "ctx", 2)
    queries, key_block, value_block, out_weight = stage(queries, key_block, value_block, out_weight)
    for own, moved in ((key_block, keys), (value_block, values)):
        for level in range(2, levels):
            hop = 1 << (level - 1)
            moved[level] = cycle(moved[level - 1], "ctx", hop, hop)
        moved[0] = swapped(jnp.where(odd, moved[1], own), "ctx")
    rest = [0] + list(range(2, levels))
    piece = count // CHUNKS

    arrived = [[] for _ in range(CHUNKS)]
    for turn in range(1, groups):
        route = [(i, ((i // 2 + turn) % groups) * 2 + i % 2) for i in range(kvh_size)]
        (state,) = call(
            "early", scale, [None, 1], turn, 0, count, block_valid, queries, None, None,
            [key_block, keys[1]], [value_block, values[1]],
        )
        for j in range(CHUNKS):
            send, keep = call(
                "late", scale, rest, turn, j * piece, piece, block_valid, queries, state, out_weight,
                [keys[i] for i in rest], [values[i] for i in rest],
            )
            got = swapped(send, "kvh")
            both = (keep.astype(F32) + got.astype(F32)).astype(BF16)
            arrived[j].append(lax.ppermute(both, "kvh", route))
    send, keep = call(
        "full", scale, [None, 1] + rest, 0, 0, count, block_valid, queries, None, out_weight,
        [key_block, keys[1]] + [keys[i] for i in rest], [value_block, values[1]] + [values[i] for i in rest],
    )
    got = swapped(send, "kvh")
    return finish(keep, got, [x[0] if len(x) == 1 else jnp.concatenate(x, axis=1) for x in arrived])


def solution(mesh):
    return jax.shard_map(
        per_device,
        mesh=mesh,
        in_specs=(P("ctx", "kvh"), P("ctx", "kvh"), P("ctx", "kvh"), P(), P("kvh", None)),
        out_specs=P(("ctx", "kvh"), None),
        check_vma=False,
    )
```

time: 126 us -> 63.6 us (0.50)
  the two profiles are of different devices: /device:TPU:0 before, /device:TPU:8 now
where the time goes in v1:
time: 63.6 us; the launch traced here: 63.3 us
  Pallas kernels  22 us (35%)
  waiting for transfers between devices  21.3 us (33%)
  starting transfers between devices  13.8 us (22%)
  local copies, waits for them, and re-layouts  5.81 us (9%)
    ppermute x2, waiting for transfers between devices, per_device(): arrived[j].append(lax.ppermute(both, 'kvh', route))  20.5 us
    pallas_call x4, Pallas kernels, call(): pl.pallas_call(functools.partial(kernel_body, mode, scale, levels, turn,...  19.6 us
    ppermute x4, starting transfers between devices, cycle(): lax.ppermute(block, axis, [(first + i, first + (i + distance) % count) fo...  8.76 us
    unnamed x10, local copies, waits for them, and re-layouts  5.81 us
    ppermute x5, starting transfers between devices, swapped(): lax.ppermute(block, axis, [(i, i ^ 1) for i in range(lax.axis_size(axis))])  2.87 us
    ppermute x2, starting transfers between devices, per_device(): arrived[j].append(lax.ppermute(both, 'kvh', route))  2.16 us
  transfers between devices with their start and end apart: 11, of which 3 were waited for; matrix products, arithmetic and copies ran while one was open for 0% of the time, Pallas kernels for 28%

profile of v1, /device:TPU:8, one launch (start us, length us, event | category | flops | bytes accessed | tf_op | source)
XLA Modules:
  0.0 63.3 jit_solution(8313275737314616818)
XLA Ops:
  0.0 0.0 copy-start.4
  0.0 1.6 %collective-permute-start.3 = (bf16[512,128]{1,0:T(8,128)(2,1)}, bf16[512,128]{1,0:T(8,128)(2,1)S(1)}, u32[]{:S(2)}, u32[]{:S(2)}) collective-permute-start(bf16[512,128]{1,0:T(8,128)(2,1)} %refs_2_.1), channel_id=1, source_target_pairs={{0,8},{4,12},{8,16},{12,20},{16,24},{20,28},{24,0},{28,4},{1,9},{5... | collective-permute-start | bytes 393224 | tf_op jit(solution)/shard_map/ppermute | solution.py:228
  1.6 1.6 %collective-permute-start = (bf16[512,128]{1,0:T(8,128)(2,1)}, bf16[512,128]{1,0:T(8,128)(2,1)S(1)}, u32[]{:S(2)}, u32[]{:S(2)}) collective-permute-start(bf16[512,128]{1,0:T(8,128)(2,1)} %refs_1_.1), channel_id=1, source_target_pairs={{0,8},{4,12},{8,16},{12,20},{16,24},{20,28},{24,0},{28,4},{1,9},{5... | collective-permute-start | bytes 393224 | tf_op jit(solution)/shard_map/ppermute | solution.py:228
  3.2 0.0 copy-start
  3.2 2.8 %copy-done = bf16[896,3584]{1,0:T(8,128)(2,1)S(1)} copy-done((bf16[896,3584]{1,0:T(8,128)(2,1)S(1)}, bf16[896,3584]{1,0:T(8,128)(2,1)}, u32[]{:S(2)}) %copy-start) | copy-done | bytes 6422552
  6.0 0.0 copy-start.1
  6.0 1.2 %copy-done.1 = bf16[512,896]{1,0:T(8,128)(2,1)S(1)} copy-done((bf16[512,896]{1,0:T(8,128)(2,1)S(1)}, bf16[512,896]{1,0:T(8,128)(2,1)}, u32[]{:S(2)}) %copy-start.1) | copy-done | bytes 917528
  7.2 0.0 copy-start.2
  7.2 0.9 %copy-done.2 = bf16[512,128]{1,0:T(8,128)(2,1)S(1)} copy-done((bf16[512,128]{1,0:T(8,128)(2,1)S(1)}, bf16[512,128]{1,0:T(8,128)(2,1)}, u32[]{:S(2)}) %copy-start.2) | copy-done | bytes 131096
  8.1 0.0 copy-start.3
  8.1 0.9 %copy-done.3 = bf16[512,128]{1,0:T(8,128)(2,1)S(1)} copy-done((bf16[512,128]{1,0:T(8,128)(2,1)S(1)}, bf16[512,128]{1,0:T(8,128)(2,1)}, u32[]{:S(2)}) %copy-start.3) | copy-done | bytes 131096
  9.0 1.2 %stage.1 = (bf16[512,896]{1,0:T(8,128)(2,1)S(1)}, bf16[512,128]{1,0:T(8,128)(2,1)S(1)}, bf16[512,128]{1,0:T(8,128)(2,1)S(1)}, bf16[896,3584]{1,0:T(8,128)(2,1)S(1)}) custom-call(bf16[512,896]{1,0:T(8,128)(2,1)S(1)} %copy-done.1, bf16[512,128]{1,0:T(8,128)(2,1)S(1)} %copy-done.3, bf16[512,128]{1,0:T(8,128)(2,1)S(1)} %copy-done.2, bf16[896,3584]{1,0:T(8,128)(2,1)S(1)} %copy-done), custom_call_target="tpu_custom_call" | custom-call | bytes 7602176 | tf_op jit(solution)/shard_map/stage/pallas_call | solution.py:102
  10.2 0.0 collective-permute-done.3.refs_8_.refs_5_
  10.2 1.6 %collective-permute-start.4 = (bf16[512,128]{1,0:T(8,128)(2,1)S(1)}, bf16[512,128]{1,0:T(8,128)(2,1)S(1)}, u32[]{:S(2)}, u32[]{:S(2)}) collective-permute-start(bf16[512,128]{1,0:T(8,128)(2,1)S(1)} %broadcast_select_fusion), channel_id=1, source_target_pairs={{0,4},{4,0},{8,12},{12,8},{16,20},{20,16},{24,28},{28,24},{1,5},{5... | collective-permute-start | bytes 393224 | tf_op jit(solution)/shard_map/ppermute | solution.py:234
  11.8 0.0 collective-permute-done.refs_4_.refs_3_
  11.8 0.6 collective-permute-start.1
  12.4 1.9 %collective-permute-start.2 = (bf16[512,128]{1,0:T(8,128)(2,1)S(1)}, bf16[512,128]{1,0:T(8,128)(2,1)S(1)}, u32[]{:S(2)}, u32[]{:S(2)}) collective-permute-start(bf16[512,128]{1,0:T(8,128)(2,1)S(1)} %collective-permute-done.refs_4_.refs_3_), channel_id=1, source_target_pairs={{8,16},{12,20},{16,24},{20,28},{24,8},{28,12},{9,17},{13,21},{17,2... | collective-permute-start | bytes 393224 | tf_op jit(solution)/shard_map/ppermute | solution.py:228
  14.3 3.7 %collective-permute-start.5 = (bf16[512,128]{1,0:T(8,128)(2,1)S(1)}, bf16[512,128]{1,0:T(8,128)(2,1)S(1)}, u32[]{:S(2)}, u32[]{:S(2)}) collective-permute-start(bf16[512,128]{1,0:T(8,128)(2,1)S(1)} %collective-permute-done.3.refs_8_.refs_5_), channel_id=1, source_target_pairs={{8,16},{12,20},{16,24},{20,28},{24,8},{28,12},{9,17},{13,21},{17,2... | collective-permute-start | bytes 393224 | tf_op jit(solution)/shard_map/ppermute | solution.py:228
  18.0 0.0 copy-done.4
  18.0 3.8 %shard_map.56.refs_1_ = f32[2,7,128,256]{3,2,1,0:T(8,128)S(1)} custom-call(s32[8]{0:T(128)S(1)} %copy-done.4, bf16[512,896]{1,0:T(8,128)(2,1)S(1)} %get-tuple-element.15.refs_1_.refs_0_, bf16[512,128]{1,0:T(8,128)(2,1)S(1)} %get-tuple-element.17.refs_3_.refs_2_, bf16[512,128]{1,0:T(8,128)(2,1)S(1)} %collective-permute-done.refs_4_.refs_3_, ...), custom_call_target="tpu_custom_call" | custom-call | flops 939524096 | bytes 1441792 | tf_op jit(solution)/shard_map/pallas_call | solution.py:186
  21.8 0.0 collective-permute-done.4.refs_9_.refs_5_
  21.8 0.0 collective-permute-done.1.refs_5_.refs_3_
  21.9 0.0 collective-permute-done.2.refs_6_.refs_4_
  21.9 0.8 %collective-permute-done.5.refs_10_.refs_6_ = bf16[512,128]{1,0:T(8,128)(2,1)S(1)} collective-permute-done((bf16[512,128]{1,0:T(8,128)(2,1)S(1)}, bf16[512,128]{1,0:T(8,128)(2,1)S(1)}, u32[]{:S(2)}, u32[]{:S(2)}) %collective-permute-start.5) | collective-permute-done | bytes 131104 | tf_op jit(solution)/shard_map/ppermute | solution.py:228
  22.7 3.3 %shard_map.58 = (bf16[64,3584]{1,0:T(8,128)(2,1)S(1)}, bf16[64,3584]{1,0:T(8,128)(2,1)S(1)}) custom-call(bf16[512,896]{1,0:T(8,128)(2,1)S(1)} %get-tuple-element.15.refs_1_.refs_0_, f32[2,7,128,256]{3,2,1,0:T(8,128)S(1)} %shard_map.56.refs_1_, bf16[896,3584]{1,0:T(8,128)(2,1)S(1)} %get-tuple-element.16.refs_2_, ...), custom_call_target="tpu_custom_call" | custom-call | flops 1291845632 | bytes 9699328 | tf_op jit(solution)/shard_map/pallas_call | solution.py:186
  26.0 0.1 collective-permute-start.9
  26.1 3.3 %shard_map.57 = (bf16[64,3584]{1,0:T(8,128)(2,1)S(1)}, bf16[64,3584]{1,0:T(8,128)(2,1)S(1)}) custom-call(bf16[512,896]{1,0:T(8,128)(2,1)S(1)} %get-tuple-element.15.refs_1_.refs_0_, f32[2,7,128,256]{3,2,1,0:T(8,128)S(1)} %shard_map.56.refs_1_, bf16[896,3584]{1,0:T(8,128)(2,1)S(1)} %get-tuple-element.16.refs_2_, ...), custom_call_target="tpu_custom_call" | custom-call | flops 1291845632 | bytes 9699328 | tf_op jit(solution)/shard_map/pallas_call | solution.py:186
  29.4 0.6 collective-permute-start.7
  30.0 9.1 %shard_map.55 = (bf16[128,3584]{1,0:T(8,128)(2,1)S(1)}, bf16[128,3584]{1,0:T(8,128)(2,1)S(1)}) custom-call(s32[8]{0:T(128)S(1)} %copy-done.4, bf16[512,896]{1,0:T(8,128)(2,1)S(1)} %get-tuple-element.15.refs_1_.refs_0_, bf16[896,3584]{1,0:T(8,128)(2,1)S(1)} %get-tuple-element.16.refs_2_, bf16[512,128]{1,0:T(8,128)(2,1)S(1)} %get-tuple-element.17.refs_3_.refs_2_, ...), custom_call_target="tpu_custom_call" | custom-call | flops 3523215360 | bytes 8388608 | tf_op jit(solution)/shard_map/pallas_call | solution.py:186
  39.1 0.1 collective-permute-start.6
  39.2 0.0 collective-permute-done.9
  39.2 0.1 add_convert_fusion
  39.3 1.6 %collective-permute-start.10 = (bf16[64,3584]{1,0:T(8,128)(2,1)S(1)}, bf16[64,3584]{1,0:T(8,128)(2,1)S(1)}, u32[]{:S(2)}, u32[]{:S(2)}) collective-permute-start(bf16[64,3584]{1,0:T(8,128)(2,1)S(1)} %add_convert_fusion), channel_id=1, source_target_pairs={{0,2},{1,3},{2,0},{3,1},{4,6},{5,7},{6,4},{7,5},{8,10},{9,11},{10,... | collective-permute-start | bytes 1376264 | tf_op jit(solution)/shard_map/ppermute | solution.py:274
  40.8 0.0 collective-permute-done.7
  40.8 0.1 add_convert_fusion.1
  40.9 0.6 collective-permute-start.8
  41.6 11.2 %collective-permute-done.10.refs_1_ = bf16[64,3584]{1,0:T(8,128)(2,1)S(1)} collective-permute-done((bf16[64,3584]{1,0:T(8,128)(2,1)S(1)}, bf16[64,3584]{1,0:T(8,128)(2,1)S(1)}, u32[]{:S(2)}, u32[]{:S(2)}) %collective-permute-start.10) | collective-permute-done | bytes 458784 | tf_op jit(solution)/shard_map/ppermute | solution.py:274
  52.7 9.3 %collective-permute-done.8.refs_0_ = bf16[64,3584]{1,0:T(8,128)(2,1)S(1)} collective-permute-done((bf16[64,3584]{1,0:T(8,128)(2,1)S(1)}, bf16[64,3584]{1,0:T(8,128)(2,1)S(1)}, u32[]{:S(2)}, u32[]{:S(2)}) %collective-permute-start.8) | collective-permute-done | bytes 458784 | tf_op jit(solution)/shard_map/ppermute | solution.py:274
  62.1 0.0 collective-permute-done.6.got_ref
  62.1 1.3 %finish.1 = bf16[128,3584]{1,0:T(8,128)(2,1)} custom-call(bf16[128,3584]{1,0:T(8,128)(2,1)S(1)} %get-tuple-element.19.keep_ref, bf16[128,3584]{1,0:T(8,128)(2,1)S(1)} %collective-permute-done.6.got_ref, bf16[64,3584]{1,0:T(8,128)(2,1)S(1)} %collective-permute-done.8.refs_0_, bf16[64,3584]{1,0:T(8,128)(2,1)S(1)} %collective-permute-done.10.refs_1_), custom_call_target="tpu_custom_call" | custom-call | flops 1376256 | bytes 3670016 | tf_op jit(solution)/shard_map/finish/pallas_call | solution.py:215
  (2 shorter events, 0.0 us)
Async XLA Ops:
  0.0 18.0 %copy-start.4 = (s32[8]{0:T(128)S(1)}, s32[8]{0:T(128)}, u32[]{:S(2)}) copy-start(s32[8]{0:T(128)} %refs_0_.5) | copy-start | bytes 100
  0.0 10.2 %collective-permute-start.3 = (bf16[512,128]{1,0:T(8,128)(2,1)}, bf16[512,128]{1,0:T(8,128)(2,1)S(1)}, u32[]{:S(2)}, u32[]{:S(2)}) collective-permute-start(bf16[512,128]{1,0:T(8,128)(2,1)} %refs_2_.1), channel_id=1, source_target_pairs={{0,8},{4,12},{8,16},{12,20},{16,24},{20,28},{24,0},{28,4},{1,9},{5... | collective-permute-start | bytes 393224 | tf_op jit(solution)/shard_map/ppermute | solution.py:228
  1.6 10.2 %collective-permute-start = (bf16[512,128]{1,0:T(8,128)(2,1)}, bf16[512,128]{1,0:T(8,128)(2,1)S(1)}, u32[]{:S(2)}, u32[]{:S(2)}) collective-permute-start(bf16[512,128]{1,0:T(8,128)(2,1)} %refs_1_.1), channel_id=1, source_target_pairs={{0,8},{4,12},{8,16},{12,20},{16,24},{20,28},{24,0},{28,4},{1,9},{5... | collective-permute-start | bytes 393224 | tf_op jit(solution)/shard_map/ppermute | solution.py:228
  3.2 2.8 %copy-start = (bf16[896,3584]{1,0:T(8,128)(2,1)S(1)}, bf16[896,3584]{1,0:T(8,128)(2,1)}, u32[]{:S(2)}) copy-start(bf16[896,3584]{1,0:T(8,128)(2,1)} %refs_3_.1) | copy-start | bytes 19267588
  6.0 1.2 %copy-start.1 = (bf16[512,896]{1,0:T(8,128)(2,1)S(1)}, bf16[512,896]{1,0:T(8,128)(2,1)}, u32[]{:S(2)}) copy-start(bf16[512,896]{1,0:T(8,128)(2,1)} %refs_0_.3) | copy-start | bytes 2752516
  7.2 0.9 %copy-start.2 = (bf16[512,128]{1,0:T(8,128)(2,1)S(1)}, bf16[512,128]{1,0:T(8,128)(2,1)}, u32[]{:S(2)}) copy-start(bf16[512,128]{1,0:T(8,128)(2,1)} %refs_2_.1) | copy-start | bytes 393220
  8.1 0.9 %copy-start.3 = (bf16[512,128]{1,0:T(8,128)(2,1)S(1)}, bf16[512,128]{1,0:T(8,128)(2,1)}, u32[]{:S(2)}) copy-start(bf16[512,128]{1,0:T(8,128)(2,1)} %refs_1_.1) | copy-start | bytes 393220
  10.2 11.6 %collective-permute-start.4 = (bf16[512,128]{1,0:T(8,128)(2,1)S(1)}, bf16[512,128]{1,0:T(8,128)(2,1)S(1)}, u32[]{:S(2)}, u32[]{:S(2)}) collective-permute-start(bf16[512,128]{1,0:T(8,128)(2,1)S(1)} %broadcast_select_fusion), channel_id=1, source_target_pairs={{0,4},{4,0},{8,12},{12,8},{16,20},{20,16},{24,28},{28,24},{1,5},{5... | collective-permute-start | bytes 393224 | tf_op jit(solution)/shard_map/ppermute | solution.py:234
  11.8 10.0 %collective-permute-start.1 = (bf16[512,128]{1,0:T(8,128)(2,1)S(1)}, bf16[512,128]{1,0:T(8,128)(2,1)S(1)}, u32[]{:S(2)}, u32[]{:S(2)}) collective-permute-start(bf16[512,128]{1,0:T(8,128)(2,1)S(1)} %broadcast_select_fusion.1), channel_id=1, source_target_pairs={{0,4},{4,0},{8,12},{12,8},{16,20},{20,16},{24,28},{28,24},{1,5},{5... | collective-permute-start | bytes 393224 | tf_op jit(solution)/shard_map/ppermute | solution.py:234
  12.4 9.5 %collective-permute-start.2 = (bf16[512,128]{1,0:T(8,128)(2,1)S(1)}, bf16[512,128]{1,0:T(8,128)(2,1)S(1)}, u32[]{:S(2)}, u32[]{:S(2)}) collective-permute-start(bf16[512,128]{1,0:T(8,128)(2,1)S(1)} %collective-permute-done.refs_4_.refs_3_), channel_id=1, source_target_pairs={{8,16},{12,20},{16,24},{20,28},{24,8},{28,12},{9,17},{13,21},{17,2... | collective-permute-start | bytes 393224 | tf_op jit(solution)/shard_map/ppermute | solution.py:228
  14.3 8.3 %collective-permute-start.5 = (bf16[512,128]{1,0:T(8,128)(2,1)S(1)}, bf16[512,128]{1,0:T(8,128)(2,1)S(1)}, u32[]{:S(2)}, u32[]{:S(2)}) collective-permute-start(bf16[512,128]{1,0:T(8,128)(2,1)S(1)} %collective-permute-done.3.refs_8_.refs_5_), channel_id=1, source_target_pairs={{8,16},{12,20},{16,24},{20,28},{24,8},{28,12},{9,17},{13,21},{17,2... | collective-permute-start | bytes 393224 | tf_op jit(solution)/shard_map/ppermute | solution.py:228
  26.0 13.2 %collective-permute-start.9 = (bf16[64,3584]{1,0:T(8,128)(2,1)S(1)}, bf16[64,3584]{1,0:T(8,128)(2,1)S(1)}, u32[]{:S(2)}, u32[]{:S(2)}) collective-permute-start(bf16[64,3584]{1,0:T(8,128)(2,1)S(1)} %get-tuple-element.24), channel_id=1, source_target_pairs={{0,1},{1,0},{2,3},{3,2},{4,5},{5,4},{6,7},{7,6},{8,9},{9,8},{10,11... | collective-permute-start | bytes 1376264 | tf_op jit(solution)/shard_map/ppermute | solution.py:234
  29.4 11.4 %collective-permute-start.7 = (bf16[64,3584]{1,0:T(8,128)(2,1)S(1)}, bf16[64,3584]{1,0:T(8,128)(2,1)S(1)}, u32[]{:S(2)}, u32[]{:S(2)}) collective-permute-start(bf16[64,3584]{1,0:T(8,128)(2,1)S(1)} %get-tuple-element.22), channel_id=1, source_target_pairs={{0,1},{1,0},{2,3},{3,2},{4,5},{5,4},{6,7},{7,6},{8,9},{9,8},{10,11... | collective-permute-start | bytes 1376264 | tf_op jit(solution)/shard_map/ppermute | solution.py:234
  39.1 23.0 %collective-permute-start.6 = (bf16[128,3584]{1,0:T(8,128)(2,1)S(1)}, bf16[128,3584]{1,0:T(8,128)(2,1)S(1)}, u32[]{:S(2)}, u32[]{:S(2)}) collective-permute-start(bf16[128,3584]{1,0:T(8,128)(2,1)S(1)} %get-tuple-element.20), channel_id=1, source_target_pairs={{0,1},{1,0},{2,3},{3,2},{4,5},{5,4},{6,7},{7,6},{8,9},{9,8},{10,11... | collective-permute-start | bytes 2752520 | tf_op jit(solution)/shard_map/ppermute | solution.py:234
  39.3 13.5 %collective-permute-start.10 = (bf16[64,3584]{1,0:T(8,128)(2,1)S(1)}, bf16[64,3584]{1,0:T(8,128)(2,1)S(1)}, u32[]{:S(2)}, u32[]{:S(2)}) collective-permute-start(bf16[64,3584]{1,0:T(8,128)(2,1)S(1)} %add_convert_fusion), channel_id=1, source_target_pairs={{0,2},{1,3},{2,0},{3,1},{4,6},{5,7},{6,4},{7,5},{8,10},{9,11},{10,... | collective-permute-start | bytes 1376264 | tf_op jit(solution)/shard_map/ppermute | solution.py:274
  40.9 21.1 %collective-permute-start.8 = (bf16[64,3584]{1,0:T(8,128)(2,1)S(1)}, bf16[64,3584]{1,0:T(8,128)(2,1)S(1)}, u32[]{:S(2)}, u32[]{:S(2)}) collective-permute-start(bf16[64,3584]{1,0:T(8,128)(2,1)S(1)} %add_convert_fusion.1), channel_id=1, source_target_pairs={{0,2},{1,3},{2,0},{3,1},{4,6},{5,7},{6,4},{7,5},{8,10},{9,11},{10,... | collective-permute-start | bytes 1376264 | tf_op jit(solution)/shard_map/ppermute | solution.py:274
